TPU v7x, 512 devices: a whole 4x4x16 slice. The times are simulated.
512 devices in a mesh: grp: 16 (over y, x), dev: 32 (over z, core).
Axes of the slice: x: 4, y: 4, z: 16, core: 2. Of those that a mesh axis runs over, the one named last changes fastest.
Arguments:
- points: float32 [3, 524288], P(None, ('grp', 'dev')), may hold values from 0 to 2
- charges: float32 [16, 524288], P(None, ('grp', 'dev')), may hold values from -6 to 6
- morton: int32 [524288], P(('grp', 'dev')), may hold values from 0 to 1023, as said below
- neighbours: int32 [2048, 8], P(('grp', 'dev')), may hold values from 0 to 2047, as said below
- counts: int32 [2048], P(('grp', 'dev')), may hold values from 1 to 8
- skel_leaf: float32 [3, 524288], P(None, ('grp', 'dev')), may hold values from 0 to 2
- skel_block: float32 [3, 131072], P(None, ('grp', 'dev')), may hold values from 0 to 2
- skel_group: float32 [3, 4096], replicated, may hold values from 0 to 2
Outputs:
- potential: float32 [16, 524288], P(None, ('grp', 'dev'))
Inputs may be any that keep to these rules, and one draw needn't show every extreme that they name: `morton`: each aligned run of 1024 entries is a permutation of 0 to 1023. `neighbours`: entry [q, k] is a leaf other than q, at most 4 leaves away from q; only slots k < counts[q] are used.
All inputs are finite; a program needn't handle non-finite values.
Results may differ from a plain program's by a relative error of at most 0.0003.
Values sent between devices are 32-bit elements; how exact they have to be, the bound alone decides.
No kernel may reach another device: no remote copies, remote signals or barrier semaphores. Data moves between devices by JAX's collectives and lax.ppermute only.
A program may use at most 64 MiB of HBM per device.

v0:
```python
import math
import jax
import jax.numpy as jnp
from jax import lax
from jax.sharding import PartitionSpec as P

width_sq = 0.1
gain_factor = 5.0


def extended_2(cells, sides, width):
    for axis, dim in sides:
        count = lax.axis_size(axis)
        ends = count - 1
        head = lax.slice_in_dim(cells, 0, width, axis=dim)
        tail = lax.slice_in_dim(cells, cells.shape[dim] - width, cells.shape[dim], axis=dim)
        cells = jnp.concatenate(
            [
                lax.ppermute(tail, axis, [(i, (i + 1) % count) for i in range(ends)]),
                cells,
                lax.ppermute(head, axis, [((i + 1) % count, i) for i in range(ends)]),
            ],
            axis=dim,
        )
    return cells


def kernel_tile(source, target):
    distance = (source[0][:, None] - target[0][None, :]) ** 2
    distance = distance + (source[1][:, None] - target[1][None, :]) ** 2
    distance = distance + (source[2][:, None] - target[2][None, :]) ** 2
    return jnp.exp(-distance / width_sq)


def translate(values, source, target, term_count):
    product = jnp.dot(
        values,
        kernel_tile(source, target),
        precision=lax.Precision.HIGHEST,
        preferred_element_type=jnp.float32,
    )
    return gain_factor / math.sqrt(term_count) * product


def far_sum(running, weights, skeleton, target, own_member, skel_rank, term_count):
    span_cols = weights.shape[1]
    block_cols = min(skel_rank, span_cols)

    def one_block(block_index, partial_value):
        column = block_index * block_cols
        piece_w = lax.dynamic_slice_in_dim(weights, column, block_cols, 1)
        piece_s = lax.dynamic_slice_in_dim(skeleton, column, block_cols, 1)
        member = column // skel_rank
        keep_mask = jnp.where(member == own_member, 0.0, 1.0)
        return partial_value + keep_mask * translate(piece_w, piece_s, target, term_count)

    return lax.fori_loop(0, span_cols // block_cols, one_block, running)


def body(points, charges, morton, neighbours, counts, skel_leaf, skel_block, skel_group):
    n_groups = lax.axis_size("grp")
    n_blocks = lax.axis_size("dev")
    vectors, block_pts = charges.shape
    leaf_count = counts.shape[0]
    leaf_size = block_pts // leaf_count
    skel_rank = skel_block.shape[1]
    slot_total = neighbours.shape[1]
    group_id = lax.axis_index("grp")
    member_id = lax.axis_index("dev")
    block_id = group_id * n_blocks + member_id
    sorted_pts = jnp.take(points, morton, axis=1)
    sorted_chg = jnp.take(charges, morton, axis=1)
    leaf_pts = sorted_pts.reshape(3, leaf_count, leaf_size).transpose(1, 0, 2)
    leaf_chg = sorted_chg.reshape(vectors, leaf_count, leaf_size).transpose(1, 0, 2)
    leaf_skel = skel_leaf.reshape(3, leaf_count, skel_rank).transpose(1, 0, 2)
    leaf_weights = lax.map(
        lambda inputs: translate(inputs[0], inputs[1], inputs[2], leaf_size),
        (leaf_chg, leaf_pts, leaf_skel),
    )
    lifted = lax.map(
        lambda inputs: translate(inputs[0], inputs[1], skel_block, leaf_count * skel_rank),
        (leaf_weights, leaf_skel),
    )
    block_weights = jnp.sum(lifted, axis=0)
    own_group = lax.dynamic_slice_in_dim(skel_group, group_id * skel_rank, skel_rank, 1)
    raised = translate(block_weights, skel_block, own_group, n_blocks * skel_rank)
    empty = jnp.zeros((vectors, skel_rank), jnp.float32)
    group_terms = (n_groups - 1) * skel_rank
    group_weights = lax.psum(raised, "dev")
    group_field = far_sum(
        empty,
        lax.all_gather(group_weights, "grp", axis=1, tiled=True),
        skel_group,
        own_group,
        group_id,
        skel_rank,
        group_terms,
    )
    peer_field = far_sum(
        empty,
        lax.all_gather(block_weights, "dev", axis=1, tiled=True),
        lax.all_gather(skel_block, "dev", axis=1, tiled=True),
        skel_block,
        member_id,
        skel_rank,
        (n_blocks - 1) * skel_rank,
    )
    block_field = peer_field + translate(group_field, own_group, skel_block, skel_rank)
    leaf_field = lax.map(
        lambda target: translate(block_field, skel_block, target, skel_rank), leaf_skel
    )
    stacked = jnp.concatenate([sorted_pts, sorted_chg], axis=0)
    extended = extended_2(stacked, ((("grp", "dev"), 1),), block_pts)
    ext_leaves = extended.reshape(3 + vectors, 3 * leaf_count, leaf_size).transpose(1, 0, 2)
    first_leaf = block_id * leaf_count - leaf_count

    def near_leaf(inputs):
        own_pts, own_chg, own_field, own_skel, row_nbr, row_count = inputs
        direct = translate(own_chg, own_pts, own_pts, leaf_size)
        direct = direct + translate(own_field, own_skel, own_pts, skel_rank)

        def one_slot(slot_index, running):
            source = lax.dynamic_index_in_dim(
                ext_leaves, row_nbr[slot_index] - first_leaf, 0, keepdims=False
            )
            tile_term = translate(source[3:], source[:3], own_pts, leaf_size)
            return running + jnp.where(slot_index < row_count, tile_term, jnp.zeros_like(tile_term))

        return lax.fori_loop(0, slot_total, one_slot, direct)

    potential = lax.map(near_leaf, (leaf_pts, leaf_chg, leaf_field, leaf_skel, neighbours, counts))
    return potential.transpose(1, 0, 2).reshape(vectors, block_pts)


def solution(mesh):
    return jax.shard_map(
        body,
        mesh=mesh,
        in_specs=(
            P(None, ("grp", "dev")),
            P(None, ("grp", "dev")),
            P(("grp", "dev")),
            P(("grp", "dev"), None),
            P(("grp", "dev")),
            P(None, ("grp", "dev")),
            P(None, ("grp", "dev")),
            P(),
        ),
        out_specs=P(None, ("grp", "dev")),
        check_vma=False,
    )
```

profile of v0, /device:TPU:8, one launch (start us, length us, event | category | flops | bytes accessed | tf_op | source)
XLA Modules:
  0.0 328.9 jit_solution(2411669421259678028)
XLA Ops:
  0.8 0.9 copy.25
  1.7 2.8 gather_fusion.1
  5.8 2.8 gather_fusion
  9.0 12.9 %collective-permute-start.1 = (f32[19,1024]{1,0:T(8,128)S(1)}, f32[19,1024]{1,0:T(8,128)S(1)}, u32[]{:S(2)}, u32[]{:S(2)}) collective-permute-start(f32[19,1024]{1,0:T(8,128)S(1)} %pad_maximum_fusion.1), channel_id=1, source_target_pairs={{1,0},{2,1},{3,2},{4,3},{5,4},{6,5},{7,6},{8,7},{9,8},{10,9},{11,1... | collective-permute-start | bytes 233480 | tf_op jit(solution)/shard_map/ppermute | solution.py:21
  21.9 1.9 collective-permute-start
  24.6 27.1 %all_gather.10 = f32[3,8192]{1,0:T(4,128)S(1)} all-gather(f32[3,256]{1,0:T(4,128)S(1)} %copy-done), channel_id=1, replica_groups=mesh['grp'=16,'dev'=32] {'dev'}, dimensions={1}, use_global_device_ids=true | all-gather | bytes 101376 | tf_op jit(solution)/shard_map/all_gather | solution.py:102
  52.8 1.6 while.85
  54.5 1.7 while.86
  56.2 30.2 %all_gather.9 = f32[16,8192]{1,0:T(8,128)S(1)} all-gather(f32[16,256]{1,0:T(8,128)S(1)} %reduce_sum.9), channel_id=1, replica_groups=mesh['grp'=16,'dev'=32] {'dev'}, dimensions={1}, use_global_device_ids=true | all-gather | bytes 540672 | tf_op jit(solution)/shard_map/all_gather | solution.py:101
  88.3 90.3 %psum.7 = f32[16,256]{1,0:T(8,128)S(1)} all-reduce(f32[16,256]{1,0:T(8,128)S(1)} %convolution_multiply_fusion.7), channel_id=1, replica_groups=mesh['grp'=16,'dev'=32] {'dev'}, use_global_device_ids=true, to_apply=%region_7.8 | all-reduce | flops 4096 | bytes 32768 | tf_op jit(solution)/shard_map/psum | solution.py:89
  178.7 24.5 %all_gather.11 = f32[16,4096]{1,0:T(8,128)S(1)} all-gather(f32[16,256]{1,0:T(8,128)S(1)} %psum.7), channel_id=1, replica_groups=mesh['grp'=16,'dev'=32] {'grp'}, dimensions={1}, use_global_device_ids=true | all-gather | bytes 278528 | tf_op jit(solution)/shard_map/all_gather | solution.py:92
  203.1 21.3 %while.91 = (s32[]{:T(128)}, f32[16,256]{1,0:T(8,128)S(1)}, f32[16,4096]{1,0:T(8,128)S(1)}, f32[3,4096]{1,0:T(4,128)}, f32[3,256]{1,0:T(4,128)S(1)}, /*index=5*/...) while((s32[]{:T(128)}, f32[16,256]{1,0:T(8,128)S(1)}, ...), condition=%wide.region_9.10_spmd.clone, body=%wide.region_8.9_spmd.clone.sunk | while | flops 13250586 | bytes 68032 | solution.py:57
  203.1 0.9 constant_dynamic-slice_fusion.38
  204.5 0.9 constant_dynamic-slice_fusion.38
  207.1 0.9 constant_dynamic-slice_fusion.38
  209.8 0.9 constant_dynamic-slice_fusion.38
  211.1 0.9 constant_dynamic-slice_fusion.38
  224.4 17.1 %while.90 = (s32[]{:T(128)}, f32[16,256]{1,0:T(8,128)S(1)}, f32[16,8192]{1,0:T(8,128)S(1)}, f32[3,8192]{1,0:T(4,128)S(1)}, f32[3,256]{1,0:T(4,128)S(1)}, /*index...) while((s32[]{:T(128)}, f32[16,256]{1,0:T(8,128)S(1)}, ...), condition=%wide.region_6.7_spmd.clone, body=%wide.region_5.6_spmd.clone.sunk | while | flops 13250586 | bytes 68032 | solution.py:57
  241.9 1.8 while.87
  244.7 83.6 %while.89 = (s32[]{:T(128)}, f32[4,16,256]{2,1,0:T(8,128)S(1)}, f32[4,16,256]{2,1,0:T(8,128)S(1)}, f32[4,3,256]{2,1,0:T(4,128)S(1)}, f32[4,16,256]{2,1,0:T(8,128...) while((s32[]{:T(128)}, f32[4,16,256]{2,1,0:T(8,128)S(1)}, ...), condition=%wide.region_15.16_spmd, body=%wide.region_12.15_spmd.sunk | while | flops 39735312 | bytes 213682 | solution.py:131
  246.8 18.8 %while.92 = (s32[]{:T(128)}, f32[16,256]{1,0:T(8,128)S(1)}, s32[]{:T(128)}, s32[8]{0:T(128)S(1)}, s32[]{:T(128)}, /*index=5*/f32[12,19,256]{2,1,0:T(8,128)S(1)},...) while((s32[]{:T(128)}, f32[16,256]{1,0:T(8,128)S(1)}, ...), condition=%wide.region_14.14_spmd, body=%wide.region_13.13_spmd.sunk | while | flops 13250570 | bytes 67841 | solution.py:129
  267.6 18.8 %while.92 = (s32[]{:T(128)}, f32[16,256]{1,0:T(8,128)S(1)}, s32[]{:T(128)}, s32[8]{0:T(128)S(1)}, s32[]{:T(128)}, /*index=5*/f32[12,19,256]{2,1,0:T(8,128)S(1)},...) while((s32[]{:T(128)}, f32[16,256]{1,0:T(8,128)S(1)}, ...), condition=%wide.region_14.14_spmd, body=%wide.region_13.13_spmd.sunk | while | flops 13250570 | bytes 67841 | solution.py:129
  288.5 18.8 %while.92 = (s32[]{:T(128)}, f32[16,256]{1,0:T(8,128)S(1)}, s32[]{:T(128)}, s32[8]{0:T(128)S(1)}, s32[]{:T(128)}, /*index=5*/f32[12,19,256]{2,1,0:T(8,128)S(1)},...) while((s32[]{:T(128)}, f32[16,256]{1,0:T(8,128)S(1)}, ...), condition=%wide.region_14.14_spmd, body=%wide.region_13.13_spmd.sunk | while | flops 13250570 | bytes 67841 | solution.py:129
  309.4 18.8 %while.92 = (s32[]{:T(128)}, f32[16,256]{1,0:T(8,128)S(1)}, s32[]{:T(128)}, s32[8]{0:T(128)S(1)}, s32[]{:T(128)}, /*index=5*/f32[12,19,256]{2,1,0:T(8,128)S(1)},...) while((s32[]{:T(128)}, f32[16,256]{1,0:T(8,128)S(1)}, ...), condition=%wide.region_14.14_spmd, body=%wide.region_13.13_spmd.sunk | while | flops 13250570 | bytes 67841 | solution.py:129
  (320 shorter events, 85.6 us)
Async XLA Ops:
  0.0 0.8 copy-start.3
  4.7 0.8 copy-start.2
  9.0 234.7 %collective-permute-start.1 = (f32[19,1024]{1,0:T(8,128)S(1)}, f32[19,1024]{1,0:T(8,128)S(1)}, u32[]{:S(2)}, u32[]{:S(2)}) collective-permute-start(f32[19,1024]{1,0:T(8,128)S(1)} %pad_maximum_fusion.1), channel_id=1, source_target_pairs={{1,0},{2,1},{3,2},{4,3},{5,4},{6,5},{7,6},{8,7},{9,8},{10,9},{11,1... | collective-permute-start | bytes 233480 | tf_op jit(solution)/shard_map/ppermute | solution.py:21
  21.9 221.8 %collective-permute-start = (f32[19,1024]{1,0:T(8,128)S(1)}, f32[19,1024]{1,0:T(8,128)S(1)}, u32[]{:S(2)}, u32[]{:S(2)}) collective-permute-start(f32[19,1024]{1,0:T(8,128)S(1)} %pad_maximum_fusion.1), channel_id=1, source_target_pairs={{0,1},{1,2},{2,3},{3,4},{4,5},{5,6},{6,7},{7,8},{8,9},{9,10},{10,1... | collective-permute-start | bytes 233480 | tf_op jit(solution)/shard_map/ppermute | solution.py:19
  23.9 0.7 copy-start
  52.1 0.7 copy-start.1
  244.0 0.7 copy-start.4
where the time goes:
time: 331 us; the launch traced here: 329 us
  blocking collectives  172 us (52%)
  local copies, waits for them, and re-layouts  55.4 us (17%)
  loops' own time  45.1 us (14%)
  matrix products  39.9 us (12%)
  starting transfers between devices  14.8 us (4%)
    psum x1, blocking collectives, body(): group_weights = lax.psum(raised, 'dev')  90.3 us
    another operation x4, loops' own time, near_leaf(): return lax.fori_loop(0, slot_total, one_slot, direct)  41.7 us
    dot_general x102, matrix products, translate(): jnp.dot(values, kernel_tile(source, target), precision=lax.Precision.HIGH...  39.9 us
    all_gather x1, blocking collectives, body(): lax.all_gather(block_weights, 'dev', axis=1, tiled=True)  30.2 us
    all_gather x1, blocking collectives, body(): lax.all_gather(skel_block, 'dev', axis=1, tiled=True)  27.1 us
    all_gather x1, blocking collectives, body(): lax.all_gather(group_weights, 'grp', axis=1, tiled=True)  24.5 us
    dynamic_slice x32, local copies, waits for them, and re-layouts, one_slot(): row_nbr[slot_index] - first_leaf  19.9 us
    slice x138, local copies, waits for them, and re-layouts, kernel_tile(): distance = (source[0][:, None] - target[0][None, :]) ** 2  18.6 us
  transfers between devices with their start and end apart: 2, of which 0 were waited for; matrix products, arithmetic and copies ran while one was open for 13% of the time, Pallas kernels for 0%

commit v1 on v0

--- a/solution.py
+++ b/solution.py
@@ -86,7 +86,11 @@
     raised = translate(block_weights, skel_block, own_group, n_blocks * skel_rank)
     empty = jnp.zeros((vectors, skel_rank), jnp.float32)
     group_terms = (n_groups - 1) * skel_rank
-    group_weights = lax.psum(raised, "dev")
+    group_weights = raised
+    for hop in (1, 2, 4, 8, 16):
+        group_weights = group_weights + lax.ppermute(
+            group_weights, "dev", [(dev, dev ^ hop) for dev in range(32)]
+        )
     group_field = far_sum(
         empty,
         lax.all_gather(group_weights, "grp", axis=1, tiled=True),

time: 331 us -> 272 us (0.82)
  blocking collectives: 172 us -> 84.8 us
  starting transfers between devices: 14.8 us -> 31.5 us
  waiting for transfers between devices: 0.01 us -> 12.5 us
    psum x1 -> x0, blocking collectives: 90.3 us -> none  [body(): group_weights = lax.psum(raised, 'dev')]
    ppermute x0 -> x5, starting transfers between devices: none -> 16.6 us  [body(): lax.ppermute(group_weights, 'dev', [(dev, dev ^ hop) for dev in range(32)])]
    ppermute x0 -> x5, waiting for transfers between devices: none -> 12.5 us  [body(): lax.ppermute(group_weights, 'dev', [(dev, dev ^ hop) for dev in range(32)])]
  transfers between devices with their start and end apart: 2 -> 7, of which waited for: 0 -> 2; matrix products, arithmetic and copies ran while one was open for 13% -> 8% of each run, Pallas kernels for 0% -> 0%
where the time goes in v1:
time: 272 us; the launch traced here: 270 us
  blocking collectives  84.8 us (31%)
  local copies, waits for them, and re-layouts  55.5 us (20%)
  loops' own time  44.7 us (16%)
  matrix products  39.9 us (15%)
  starting transfers between devices  31.5 us (12%)
  waiting for transfers between devices  12.5 us (5%)
    another operation x4, loops' own time, near_leaf(): return lax.fori_loop(0, slot_total, one_slot, direct)  41.3 us
    dot_general x102, matrix products, translate(): jnp.dot(values, kernel_tile(source, target), precision=lax.Precision.HIGH...  39.9 us
    all_gather x1, blocking collectives, body(): lax.all_gather(block_weights, 'dev', axis=1, tiled=True)  30.3 us
    all_gather x1, blocking collectives, body(): lax.all_gather(skel_block, 'dev', axis=1, tiled=True)  29.1 us
    all_gather x1, blocking collectives, body(): lax.all_gather(group_weights, 'grp', axis=1, tiled=True)  25.4 us
    dynamic_slice x32, local copies, waits for them, and re-layouts, one_slot(): row_nbr[slot_index] - first_leaf  19.9 us
    slice x138, local copies, waits for them, and re-layouts, kernel_tile(): distance = (source[0][:, None] - target[0][None, :]) ** 2  18.6 us
    ppermute x5, starting transfers between devices, body(): lax.ppermute(group_weights, 'dev', [(dev, dev ^ hop) for dev in range(32)])  16.6 us
  transfers between devices with their start and end apart: 7, of which 2 were waited for; matrix products, arithmetic and copies ran while one was open for 8% of the time, Pallas kernels for 0%

profile of v1, /device:TPU:8, one launch (start us, length us, event | category | flops | bytes accessed | tf_op | source)
XLA Modules:
  0.0 270.4 jit_solution(9075619175361322617)
XLA Ops:
  1.7 2.8 %gather_fusion.1 = f32[1024,3]{1,0:T(8,128)S(1)} fusion(f32[3,1024]{0,1:T(8,128)S(1)} %copy.25, s32[1024]{0:T(1024)S(1)} %fusion.219), kind=kCustom, calls=%fused_computation.1 | custom fusion | bytes 28672 | tf_op jit(solution)/shard_map/jit(_take)/gather | solution.py:71
  5.8 2.8 %gather_fusion = f32[1024,16]{1,0:T(8,128)S(1)} fusion(f32[16,1024]{0,1:T(8,128)S(1)} %copy.23, s32[1024]{0:T(1024)S(1)} %fusion.219), kind=kCustom, calls=%fused_computation | custom fusion | bytes 135168 | tf_op jit(solution)/shard_map/jit(_take)/gather | solution.py:72
  9.0 12.9 %collective-permute-start.6 = (f32[19,1024]{1,0:T(8,128)S(1)}, f32[19,1024]{1,0:T(8,128)S(1)}, u32[]{:S(2)}, u32[]{:S(2)}) collective-permute-start(f32[19,1024]{1,0:T(8,128)S(1)} %pad_maximum_fusion.1), channel_id=1, source_target_pairs={{1,0},{2,1},{3,2},{4,3},{5,4},{6,5},{7,6},{8,7},{9,8},{10,9},{11,1... | collective-permute-start | bytes 233480 | tf_op jit(solution)/shard_map/ppermute | solution.py:21
  21.9 1.9 collective-permute-start.5
  25.7 1.6 while.85
  27.4 1.7 while.86
  30.4 1.9 collective-permute-start
  32.3 30.3 %all_gather.9 = f32[16,8192]{1,0:T(8,128)S(1)} all-gather(f32[16,256]{1,0:T(8,128)S(1)} %reduce_sum.9), channel_id=1, replica_groups=mesh['grp'=16,'dev'=32] {'dev'}, dimensions={1}, use_global_device_ids=true | all-gather | bytes 540672 | tf_op jit(solution)/shard_map/all_gather | solution.py:105
  62.7 1.9 collective-permute-start.1
  64.6 29.1 %all_gather.10 = f32[3,8192]{1,0:T(4,128)S(1)} all-gather(f32[3,256]{1,0:T(4,128)S(1)} %get-tuple-element.1438), channel_id=1, replica_groups=mesh['grp'=16,'dev'=32] {'dev'}, dimensions={1}, use_global_device_ids=true | all-gather | bytes 101376 | tf_op jit(solution)/shard_map/all_gather | solution.py:106
  93.7 2.2 collective-permute-start.2
  95.9 17.1 %while.90 = (s32[]{:T(128)}, f32[16,256]{1,0:T(8,128)S(1)}, f32[16,8192]{1,0:T(8,128)S(1)}, f32[3,8192]{1,0:T(4,128)S(1)}, f32[3,256]{1,0:T(4,128)S(1)}, /*index...) while((s32[]{:T(128)}, f32[16,256]{1,0:T(8,128)S(1)}, ...), condition=%wide.region_6.7_spmd.clone, body=%wide.region_5.6_spmd.clone.sunk | while | flops 13250586 | bytes 68032 | solution.py:57
  113.0 4.3 %collective-permute-start.3 = (f32[16,256]{1,0:T(8,128)S(1)}, f32[16,256]{1,0:T(8,128)S(1)}, u32[]{:S(2)}, u32[]{:S(2)}) collective-permute-start(f32[16,256]{1,0:T(8,128)S(1)} %add.285), channel_id=1, source_target_pairs={{0,8},{1,9},{2,10},{3,11},{4,12},{5,13},{6,14},{7,15},{8,0},{9,1},... | collective-permute-start | bytes 49160 | tf_op jit(solution)/shard_map/ppermute | solution.py:91
  118.0 4.6 %collective-permute-done.3 = f32[16,256]{1,0:T(8,128)S(1)} collective-permute-done((f32[16,256]{1,0:T(8,128)S(1)}, f32[16,256]{1,0:T(8,128)S(1)}, u32[]{:S(2)}, u32[]{:S(2)}) %collective-permute-start.3) | collective-permute-done | bytes 16416 | tf_op jit(solution)/shard_map/ppermute | solution.py:91
  122.6 6.3 %collective-permute-start.4 = (f32[16,256]{1,0:T(8,128)S(1)}, f32[16,256]{1,0:T(8,128)S(1)}, u32[]{:S(2)}, u32[]{:S(2)}) collective-permute-start(f32[16,256]{1,0:T(8,128)S(1)} %add.286), channel_id=1, source_target_pairs={{0,16},{1,17},{2,18},{3,19},{4,20},{5,21},{6,22},{7,23},{8,24},{9,... | collective-permute-start | bytes 49160 | tf_op jit(solution)/shard_map/ppermute | solution.py:91
  129.2 7.9 %collective-permute-done.4 = f32[16,256]{1,0:T(8,128)S(1)} collective-permute-done((f32[16,256]{1,0:T(8,128)S(1)}, f32[16,256]{1,0:T(8,128)S(1)}, u32[]{:S(2)}, u32[]{:S(2)}) %collective-permute-start.4) | collective-permute-done | bytes 16416 | tf_op jit(solution)/shard_map/ppermute | solution.py:91
  137.1 25.4 %all_gather.11 = f32[16,4096]{1,0:T(8,128)S(1)} all-gather(f32[16,256]{1,0:T(8,128)S(1)} %add.287), channel_id=1, replica_groups=mesh['grp'=16,'dev'=32] {'grp'}, dimensions={1}, use_global_device_ids=true | all-gather | bytes 278528 | tf_op jit(solution)/shard_map/all_gather | solution.py:96
  162.4 21.3 %while.91 = (s32[]{:T(128)}, f32[16,256]{1,0:T(8,128)S(1)}, f32[16,4096]{1,0:T(8,128)S(1)}, f32[3,4096]{1,0:T(4,128)}, f32[3,256]{1,0:T(4,128)S(1)}, /*index=5*/...) while((s32[]{:T(128)}, f32[16,256]{1,0:T(8,128)S(1)}, ...), condition=%wide.region_8.9_spmd.clone, body=%wide.region_7.8_spmd.clone.sunk | while | flops 13250586 | bytes 68032 | solution.py:57
  184.1 1.8 while.87
  186.6 83.2 %while.89 = (s32[]{:T(128)}, f32[4,16,256]{2,1,0:T(8,128)S(1)}, f32[4,16,256]{2,1,0:T(8,128)S(1)}, f32[4,3,256]{2,1,0:T(4,128)S(1)}, f32[4,16,256]{2,1,0:T(8,128...) while((s32[]{:T(128)}, f32[4,16,256]{2,1,0:T(8,128)S(1)}, ...), condition=%wide.region_14.15_spmd, body=%wide.region_11.14_spmd.sunk | while | flops 39735312 | bytes 213682 | solution.py:135
  188.7 18.7 %while.92 = (s32[]{:T(128)}, f32[16,256]{1,0:T(8,128)S(1)}, s32[]{:T(128)}, s32[8]{0:T(128)S(1)}, s32[]{:T(128)}, /*index=5*/f32[12,19,256]{2,1,0:T(8,128)S(1)},...) while((s32[]{:T(128)}, f32[16,256]{1,0:T(8,128)S(1)}, ...), condition=%wide.region_13.13_spmd, body=%wide.region_12.12_spmd.sunk | while | flops 13250570 | bytes 67841 | solution.py:133
  209.5 18.7 %while.92 = (s32[]{:T(128)}, f32[16,256]{1,0:T(8,128)S(1)}, s32[]{:T(128)}, s32[8]{0:T(128)S(1)}, s32[]{:T(128)}, /*index=5*/f32[12,19,256]{2,1,0:T(8,128)S(1)},...) while((s32[]{:T(128)}, f32[16,256]{1,0:T(8,128)S(1)}, ...), condition=%wide.region_13.13_spmd, body=%wide.region_12.12_spmd.sunk | while | flops 13250570 | bytes 67841 | solution.py:133
  230.3 18.7 %while.92 = (s32[]{:T(128)}, f32[16,256]{1,0:T(8,128)S(1)}, s32[]{:T(128)}, s32[8]{0:T(128)S(1)}, s32[]{:T(128)}, /*index=5*/f32[12,19,256]{2,1,0:T(8,128)S(1)},...) while((s32[]{:T(128)}, f32[16,256]{1,0:T(8,128)S(1)}, ...), condition=%wide.region_13.13_spmd, body=%wide.region_12.12_spmd.sunk | while | flops 13250570 | bytes 67841 | solution.py:133
  251.1 18.7 %while.92 = (s32[]{:T(128)}, f32[16,256]{1,0:T(8,128)S(1)}, s32[]{:T(128)}, s32[8]{0:T(128)S(1)}, s32[]{:T(128)}, /*index=5*/f32[12,19,256]{2,1,0:T(8,128)S(1)},...) while((s32[]{:T(128)}, f32[16,256]{1,0:T(8,128)S(1)}, ...), condition=%wide.region_13.13_spmd, body=%wide.region_12.12_spmd.sunk | while | flops 13250570 | bytes 67841 | solution.py:133
  (334 shorter events, 91.0 us)
Async XLA Ops:
  0.0 0.8 copy-start.3
  4.7 0.8 copy-start.2
  9.0 119.9 %collective-permute-start.6 = (f32[19,1024]{1,0:T(8,128)S(1)}, f32[19,1024]{1,0:T(8,128)S(1)}, u32[]{:S(2)}, u32[]{:S(2)}) collective-permute-start(f32[19,1024]{1,0:T(8,128)S(1)} %pad_maximum_fusion.1), channel_id=1, source_target_pairs={{1,0},{2,1},{3,2},{4,3},{5,4},{6,5},{7,6},{8,7},{9,8},{10,9},{11,1... | collective-permute-start | bytes 233480 | tf_op jit(solution)/shard_map/ppermute | solution.py:21
  21.9 107.0 %collective-permute-start.5 = (f32[19,1024]{1,0:T(8,128)S(1)}, f32[19,1024]{1,0:T(8,128)S(1)}, u32[]{:S(2)}, u32[]{:S(2)}) collective-permute-start(f32[19,1024]{1,0:T(8,128)S(1)} %pad_maximum_fusion.1), channel_id=1, source_target_pairs={{0,1},{1,2},{2,3},{3,4},{4,5},{5,6},{6,7},{7,8},{8,9},{9,10},{10,1... | collective-permute-start | bytes 233480 | tf_op jit(solution)/shard_map/ppermute | solution.py:19
  23.9 0.7 copy-start
  25.0 0.7 copy-start.1
  30.4 32.3 %collective-permute-start = (f32[16,256]{1,0:T(8,128)S(1)}, f32[16,256]{1,0:T(8,128)S(1)}, u32[]{:S(2)}, u32[]{:S(2)}) collective-permute-start(f32[16,256]{1,0:T(8,128)S(1)} %convolution_multiply_fusion.7), channel_id=1, source_target_pairs={{0,1},{1,0},{2,3},{3,2},{4,5},{5,4},{6,7},{7,6},{8,9},{9,8},{10,11... | collective-permute-start | bytes 49160 | tf_op jit(solution)/shard_map/ppermute | solution.py:91
  62.7 31.1 %collective-permute-start.1 = (f32[16,256]{1,0:T(8,128)S(1)}, f32[16,256]{1,0:T(8,128)S(1)}, u32[]{:S(2)}, u32[]{:S(2)}) collective-permute-start(f32[16,256]{1,0:T(8,128)S(1)} %add.283), channel_id=1, source_target_pairs={{0,2},{1,3},{2,0},{3,1},{4,6},{5,7},{6,4},{7,5},{8,10},{9,11},{10,... | collective-permute-start | bytes 49160 | tf_op jit(solution)/shard_map/ppermute | solution.py:91
  93.7 19.3 %collective-permute-start.2 = (f32[16,256]{1,0:T(8,128)S(1)}, f32[16,256]{1,0:T(8,128)S(1)}, u32[]{:S(2)}, u32[]{:S(2)}) collective-permute-start(f32[16,256]{1,0:T(8,128)S(1)} %add.284), channel_id=1, source_target_pairs={{0,4},{1,5},{2,6},{3,7},{4,0},{5,1},{6,2},{7,3},{8,12},{9,13},{10,... | collective-permute-start | bytes 49160 | tf_op jit(solution)/shard_map/ppermute | solution.py:91
  113.0 9.5 %collective-permute-start.3 = (f32[16,256]{1,0:T(8,128)S(1)}, f32[16,256]{1,0:T(8,128)S(1)}, u32[]{:S(2)}, u32[]{:S(2)}) collective-permute-start(f32[16,256]{1,0:T(8,128)S(1)} %add.285), channel_id=1, source_target_pairs={{0,8},{1,9},{2,10},{3,11},{4,12},{5,13},{6,14},{7,15},{8,0},{9,1},... | collective-permute-start | bytes 49160 | tf_op jit(solution)/shard_map/ppermute | solution.py:91
  122.6 14.5 %collective-permute-start.4 = (f32[16,256]{1,0:T(8,128)S(1)}, f32[16,256]{1,0:T(8,128)S(1)}, u32[]{:S(2)}, u32[]{:S(2)}) collective-permute-start(f32[16,256]{1,0:T(8,128)S(1)} %add.286), channel_id=1, source_target_pairs={{0,16},{1,17},{2,18},{3,19},{4,20},{5,21},{6,22},{7,23},{8,24},{9,... | collective-permute-start | bytes 49160 | tf_op jit(solution)/shard_map/ppermute | solution.py:91
  185.9 0.7 copy-start.4
